TPU v7x, 32 devices: a whole 2x2x4 slice. The times are simulated.
32 devices in a mesh: dp: 4 (over y, x), ctx: 8 (over z, core).
Axes of the slice: x: 2, y: 2, z: 4, core: 2. Of those that a mesh axis runs over, the one named last changes fastest.
Arguments:
- inputs: bfloat16 [4, 2048, 4096], P('dp', 'ctx'), may hold values from -6 to 6
- query_weight: bfloat16 [4096, 128], P('dp'), may hold values from -0.09375 to 0.09375
- key_weight: bfloat16 [4096, 128], P('dp'), may hold values from -0.09375 to 0.09375
- value_weight: bfloat16 [4096, 2048], P('dp'), may hold values from -0.09375 to 0.09375
- lambda_weight: bfloat16 [4096, 320], P('dp'), may hold values from -0.09375 to 0.09375
- log_decay: float32 [4, 2048, 16], P('dp', 'ctx'), may hold values from -1 to 0, as said below
- norm_gain: float32 [2048], replicated, may hold values from 0.5 to 1.5
Outputs:
- outputs: bfloat16 [4, 2048, 2048], P('dp', 'ctx')
Inputs may be any that keep to these rules, and one draw needn't show every extreme that they name: `log_decay`: entries are not positive.
All inputs are finite; a program needn't handle non-finite values.
Results may differ from a plain program's by a relative error of at most 0.0072.
Values may be sent and summed in bfloat16 or wider, within the bound.
A program may use at most 128 MiB of HBM per device.

v0:
```python
import math
import jax
import jax.numpy as jnp
from jax import lax
from jax.sharding import PartitionSpec as P

HIGHEST = lax.Precision.HIGHEST


def from_partner(block, axis, stride):
    count = lax.axis_size(axis)
    route = []
    for low in range(count):
        high = low | 1 << stride
        if high != low and high < count:
            route += [(low, high), (high, low)]
    return lax.ppermute(block, axis, route)


def level_masks(length):
    depth = length.bit_length() - 1
    token_place = jnp.arange(length, dtype=jnp.int32)
    differ = jnp.bitwise_xor(token_place[:, None], token_place[None, :])
    level = jnp.zeros((length, length), jnp.int32)
    for power in range(depth):
        level = level + (differ >= 1 << power).astype(jnp.int32)
    levels = jnp.arange(depth + 1, dtype=jnp.int32)
    return (level[None, :, :] == levels[:, None, None]).astype(jnp.float32)


def block_terms(query_rows, key_rows, value_rows, lambdas, log_decay, masks):
    length, heads = log_decay.shape
    state_dim = query_rows.shape[1]
    head_dim = value_rows.shape[1] // heads
    inner = masks.shape[0]
    weights_all = lambdas.reshape(length, heads, -1)
    cumulative = jnp.cumsum(log_decay, axis=0)
    scores = lax.dot_general(
        query_rows, key_rows, (((1,), (1,)), ((), ())), preferred_element_type=jnp.float32
    ) / math.sqrt(state_dim)
    level_weight = jnp.einsum("lts,thl->hts", masks, weights_all[:, :, :inner], precision=HIGHEST)
    token_place = jnp.arange(length, dtype=jnp.int32)
    causal = token_place[:, None] >= token_place[None, :]
    spread = jnp.transpose(cumulative)
    distance = spread[:, :, None] - spread[:, None, :]
    decay = jnp.exp(jnp.where(causal[None], distance, -jnp.inf))
    mix = (level_weight * decay * scores[None]).astype(jnp.bfloat16)
    values = value_rows.reshape(length, heads, head_dim)
    near = jnp.einsum("hts,shd->thd", mix, values, preferred_element_type=jnp.float32)
    remain = jnp.exp(cumulative[-1][None, :] - cumulative)
    keyed = (key_rows.astype(jnp.float32)[:, None, :] * remain[:, :, None]).astype(jnp.bfloat16)
    state = jnp.einsum("chs,chd->hsd", keyed, values, preferred_element_type=jnp.float32)
    total = jnp.exp(cumulative[-1])
    return (near, state, total, cumulative, weights_all)


def finish(mixed, norm_gain):
    heads = mixed.shape[-2]
    mean_square = jnp.mean(mixed * mixed, axis=-1, keepdims=True)
    return (mixed * lax.rsqrt(mean_square + 1e-05) * norm_gain.reshape(heads, -1)).astype(
        jnp.bfloat16
    )


def make_fold(tokens):

    def accumulate(totals, pieces, start):
        return tuple(
            (jnp.dot(tokens, piece, preferred_element_type=jnp.float32) for piece in pieces)
        )

    return accumulate


def zeros_for(length, weights):
    return tuple((jnp.zeros((length, weight.shape[1]), jnp.float32) for weight in weights))


def per_device(inputs, query_weight, key_weight, value_weight, lambda_weight, log_decay, norm_gain):
    tokens = inputs[0]
    decays = log_decay[0]
    length = tokens.shape[0]
    accumulate = make_fold(tokens)
    query_sum, key_sum, value_sum, lambda_sum = accumulate(
        zeros_for(length, (query_weight, key_weight, value_weight, lambda_weight)),
        (
            lax.all_gather(query_weight, "dp", axis=0, tiled=True),
            lax.all_gather(key_weight, "dp", axis=0, tiled=True),
            lax.all_gather(value_weight, "dp", axis=0, tiled=True),
            lax.all_gather(lambda_weight, "dp", axis=0, tiled=True),
        ),
        jnp.int32(0),
    )
    query_rows = query_sum.astype(jnp.bfloat16)
    key_rows = key_sum.astype(jnp.bfloat16)
    value_rows = value_sum.astype(jnp.bfloat16)
    lambdas = jax.nn.softplus(lambda_sum)
    masks = level_masks(length)
    inner = masks.shape[0]
    scale = 1.0 / math.sqrt(query_rows.shape[1])
    near, state, total, cumulative, weights_all = block_terms(
        query_rows, key_rows, value_rows, lambdas, decays, masks
    )
    index = lax.axis_index("ctx")
    bits = lax.axis_size("ctx").bit_length() - 1
    block_state = state
    block_total = total
    carry_decay = jnp.ones_like(total)
    growth = jnp.exp(cumulative)
    mixed = near
    for level_bit in range(bits):
        other_state, other_total = from_partner((block_state, block_total), "ctx", level_bit)
        upper = (index >> level_bit & 1).astype(jnp.float32)
        carried = (carry_decay[:, None, None] * other_state).astype(jnp.bfloat16)
        reach = jnp.einsum("ts,hsd->thd", query_rows, carried, preferred_element_type=jnp.float32)
        factor = weights_all[:, :, inner + level_bit] * growth * (scale * upper)
        mixed = mixed + factor[..., None] * reach
        if level_bit + 1 < bits:
            block_state = jnp.where(
                upper > 0,
                block_total[:, None, None] * other_state + block_state,
                other_total[:, None, None] * block_state + other_state,
            )
            carry_decay = jnp.where(upper > 0, other_total * carry_decay, carry_decay)
            block_total = block_total * other_total
    return finish(mixed, norm_gain).reshape(1, length, -1)


def solution(mesh):
    return jax.shard_map(
        per_device,
        mesh=mesh,
        in_specs=(
            P("dp", "ctx", None),
            P("dp", None),
            P("dp", None),
            P("dp", None),
            P("dp", None),
            P("dp", "ctx", None),
            P(),
        ),
        out_specs=P("dp", "ctx", None),
        check_vma=False,
    )
```

profile of v0, /device:TPU:0, one launch (start us, length us, event | category | flops | bytes accessed | tf_op | source)
XLA Modules:
  0.0 352.5 jit_solution(18058356890450895991)
XLA Ops:
  6.5 0.7 all-gather.11.cloned.1.call-update
  7.3 0.7 all-gather.7.cloned.1.call-update
  8.1 0.7 all-gather.5.cloned.1.call-update
  9.9 28.5 %all-gather.11.cloned.1.call-done = bf16[4096,128]{1,0:T(8,128)(2,1)} async-done(((bf16[1024,128]{1,0:T(8,128)(2,1)}), bf16[4096,128]{1,0:T(8,128)(2,1)}) %all-gather.11.cloned.1.call-update) | async-done | bytes 1048592 | tf_op jit(solution)/shard_map/all_gather | solution.py:88
  38.4 1.9 fusion.21
  40.5 39.3 %all-gather.7.cloned.1.call-done = bf16[4096,320]{0,1:T(8,128)(2,1)} async-done(((bf16[1024,320]{0,1:T(8,128)(2,1)}), bf16[4096,320]{0,1:T(8,128)(2,1)}) %all-gather.7.cloned.1.call-update) | async-done | bytes 2621456 | tf_op jit(solution)/shard_map/all_gather | solution.py:90
  79.8 2.7 compare_select_fusion
  82.6 0.7 fusion.44
  83.4 155.6 %all-gather.5.cloned.1.call-done = bf16[4096,2048]{1,0:T(8,128)(2,1)} async-done(((bf16[1024,2048]{1,0:T(8,128)(2,1)}), bf16[4096,2048]{1,0:T(8,128)(2,1)}) %all-gather.5.cloned.1.call-update) | async-done | bytes 16777232 | tf_op jit(solution)/shard_map/all_gather | solution.py:89
  239.0 8.3 %fusion.15 = bf16[32,16,8,128]{3,2,1,0:T(8,128)(2,1)S(1)} fusion(bf16[4096,2048]{1,0:T(8,128)(2,1)} %all-gather.5.cloned.1.call-done, bf16[1,256,4096]{2,1,0:T(8,128)(2,1)S(1)} %copy-done), kind=kOutput, calls=%fused_computation.22 | convolution fusion | flops 4295491584 | bytes 19922944 | tf_op jit(solution)/shard_map/dot_general | solution.py:69
  247.3 1.0 copy-done.6
  249.4 0.8 convert_add_fusion
  250.2 1.4 collective-permute-done.1
  251.5 3.0 fusion.48
  254.6 1.5 collective-permute-start.2
  257.3 0.7 copy.39
  258.0 21.9 %collective-permute-done.3 = f32[16]{0:T(128)S(1)} collective-permute-done((f32[16]{0:T(128)S(1)}, f32[16]{0:T(128)S(1)}, u32[]{:S(2)}, u32[]{:S(2)}) %collective-permute-start.3) | collective-permute-done | bytes 96 | tf_op jit(solution)/shard_map/ppermute | solution.py:17
  280.5 1.9 fusion.18
  282.4 0.9 convolution_multiply_fusion
  283.3 2.5 copy.51
  285.9 2.9 multiply_convert_fusion.4
  288.8 2.4 collective-permute-start.4
  291.3 3.6 %fusion.1 = bf16[16,256,256]{2,0,1:T(8,128)(2,1)S(1)} fusion(f32[256,16,9]{2,1,0:T(8,128)S(1)} %copy-done.3, f32[256,256]{1,0:T(8,128)S(1)} %copy-done.9, f32[16,256]{1,0:T(8,128)S(1)} %copy-done.15, f32[16,256]{0,1:T(8,128)S(1)} %copy-done.11, s32[256,256]{1,0:T(8,128)S(1)} %copy-done.10, pred[256,256]{1,0:T(8,128)(4,1)S(1)} %copy-done.16), kind=kOutput, calls=%fused_computation.2 | convolution fusion | flops 119078912 | bytes 2867200 | tf_op jit(solution)/shard_map/lts,thl->hts/dot_general | solution.py:41
  294.9 2.3 fusion.12
  297.2 1.0 copy.45
  298.2 2.8 fusion.50
  301.3 1.8 fusion.51
  303.1 34.4 %collective-permute-done.4 = f32[16,128,128]{2,1,0:T(8,128)} collective-permute-done((f32[16,128,128]{2,1,0:T(8,128)}, f32[16,128,128]{2,1,0:T(8,128)}, u32[]{:S(2)}, u32[]{:S(2)}) %collective-permute-start.4) | collective-permute-done | bytes 1048608 | tf_op jit(solution)/shard_map/ppermute | solution.py:17
  337.5 1.4 multiply_convert_fusion.3
  339.7 1.1 copy-done.1
  340.8 3.3 multiply_reduce_fusion
  344.5 1.4 copy.49
  (83 shorter events, 5.7 us)
Async XLA Ops:
  6.5 31.9 %copy-start = (bf16[1,256,4096]{2,1,0:T(8,128)(2,1)S(1)}, bf16[1,256,4096]{2,1,0:T(8,128)(2,1)}, u32[]{:S(2)}) copy-start(bf16[1,256,4096]{2,1,0:T(8,128)(2,1)} %param.7) | copy-start | bytes 6291460
  6.5 31.9 %all-gather.11.cloned.1.call-start = ((), (), s32[]{:S(2)}) async-start(), calls=%async_computation.3 | async-start | bytes 1310720 | tf_op jit(solution)/shard_map/all_gather | solution.py:88
  7.3 72.6 %all-gather.7.cloned.1.call-start = ((), (), s32[]{:S(2)}) async-start(), calls=%async_computation.1 | async-start | bytes 3276800 | tf_op jit(solution)/shard_map/all_gather | solution.py:90
  8.0 231.0 %all-gather.5.cloned.1.call-start = ((), (), s32[]{:S(2)}) async-start(), calls=%async_computation | async-start | bytes 20971520 | tf_op jit(solution)/shard_map/all_gather | solution.py:89
  8.8 271.7 %all-gather.9.cloned.1.call-start = ((), (), s32[]{:S(2)}) async-start(), calls=%async_computation.2 | async-start | bytes 1310720 | tf_op jit(solution)/shard_map/all_gather | solution.py:87
  9.7 247.6 %copy-start.14 = (f32[16,256]{1,0:T(8,128)}, f32[16,256]{1,0:T(8,128)S(1)}, u32[]{:S(2)}) copy-start(f32[16,256]{1,0:T(8,128)S(1)} %get-tuple-element.16) | copy-start | bytes 49156
  82.6 164.7 %copy-start.5 = (f32[256,16,20]{0,2,1:T(8,128)}, f32[256,16,20]{0,2,1:T(8,128)S(1)}, u32[]{:S(2)}) copy-start(f32[256,16,20]{0,2,1:T(8,128)S(1)} %reshape.113) | copy-start | bytes 983044
  247.2 1.0 copy-start.6
  248.7 2.9 copy-start.8
  248.7 2.9 collective-permute-start
  248.8 2.7 collective-permute-start.1
  251.5 5.7 %copy-start.20 = (f32[16]{0:T(128)}, f32[16]{0:T(128)S(1)}, u32[]{:S(2)}) copy-start(f32[16]{0:T(128)S(1)} %collective-permute-done.1) | copy-start | bytes 196
  254.6 31.3 %collective-permute-start.2 = (f32[16,128,128]{2,1,0:T(8,128)S(1)}, f32[16,128,128]{2,1,0:T(8,128)}, u32[]{:S(2)}, u32[]{:S(2)}) collective-permute-start(f32[16,128,128]{2,1,0:T(8,128)S(1)} %get-tuple-element.10), channel_id=1, source_target_pairs={{0,2},{2,0},{1,3},{3,1},{4,6},{6,4},{5,7},{7,5},{8,10},{10,8},{9,1... | collective-permute-start | bytes 3145736 | tf_op jit(solution)/shard_map/ppermute | solution.py:17
  256.7 23.8 %copy-start.24 = (f32[16]{0:T(128)}, f32[16]{0:T(128)S(1)}, u32[]{:S(2)}) copy-start(f32[16]{0:T(128)S(1)} %exponential_multiply_fusion) | copy-start | bytes 196
  256.7 23.2 %collective-permute-start.3 = (f32[16]{0:T(128)S(1)}, f32[16]{0:T(128)S(1)}, u32[]{:S(2)}, u32[]{:S(2)}) collective-permute-start(f32[16]{0:T(128)S(1)} %exponential_multiply_fusion), channel_id=1, source_target_pairs={{0,2},{2,0},{1,3},{3,1},{4,6},{6,4},{5,7},{7,5},{8,10},{10,8},{9,1... | collective-permute-start | bytes 200 | tf_op jit(solution)/shard_map/ppermute | solution.py:17
  258.0 25.3 %slice-start = ((f32[256,16,20]{0,2,1:T(8,128)}), f32[256,16,9]{0,2,1:T(8,128)S(1)}, s32[]{:S(2)}) async-start(f32[256,16,20]{0,2,1:T(8,128)} %copy-done.5), calls=%async_computation.4 | async-start | bytes 524288 | tf_op jit(solution)/shard_map/slice | solution.py:41
  283.3 2.6 copy-start.22
  283.3 2.6 copy-start.23
  283.3 2.6 copy-start.25
  285.9 5.4 %copy-start.3 = (f32[256,16,9]{2,1,0:T(8,128)S(1)}, f32[256,16,9]{2,1,0:T(8,128)}, u32[]{:S(2)}) copy-start(f32[256,16,9]{2,1,0:T(8,128)} %copy.51) | copy-start | bytes 442372
  285.9 5.4 %copy-start.9 = (f32[256,256]{1,0:T(8,128)S(1)}, f32[256,256]{1,0:T(8,128)}, u32[]{:S(2)}) copy-start(f32[256,256]{1,0:T(8,128)} %convolution_multiply_fusion) | copy-start | bytes 786436
  285.9 5.4 %copy-start.10 = (s32[256,256]{1,0:T(8,128)S(1)}, s32[256,256]{1,0:T(8,128)}, u32[]{:S(2)}) copy-start(s32[256,256]{1,0:T(8,128)} %convert_add_fusion) | copy-start | bytes 786436
  285.9 5.4 %copy-start.11 = (f32[16,256]{0,1:T(8,128)S(1)}, f32[16,256]{0,1:T(8,128)}, u32[]{:S(2)}) copy-start(f32[16,256]{0,1:T(8,128)} %copy.39) | copy-start | bytes 49156
  285.9 5.4 %copy-start.15 = (f32[16,256]{1,0:T(8,128)S(1)}, f32[16,256]{1,0:T(8,128)}, u32[]{:S(2)}) copy-start(f32[16,256]{1,0:T(8,128)} %copy-done.14) | copy-start | bytes 49156
  285.9 5.4 %copy-start.16 = (pred[256,256]{1,0:T(8,128)(4,1)S(1)}, pred[256,256]{1,0:T(8,128)(4,1)}, u32[]{:S(2)}) copy-start(pred[256,256]{1,0:T(8,128)(4,1)} %iota_compare_fusion.4) | copy-start | bytes 196612
  288.8 6.1 %copy-start.7 = (bf16[32,16,8,128]{3,2,1,0:T(8,128)(2,1)S(1)}, bf16[32,16,8,128]{3,2,1,0:T(8,128)(2,1)}, u32[]{:S(2)}) copy-start(bf16[32,16,8,128]{3,2,1,0:T(8,128)(2,1)} %copy-done.6) | copy-start | bytes 3145732
  288.8 48.7 %collective-permute-start.4 = (f32[16,128,128]{2,1,0:T(8,128)}, f32[16,128,128]{2,1,0:T(8,128)}, u32[]{:S(2)}, u32[]{:S(2)}) collective-permute-start(f32[16,128,128]{2,1,0:T(8,128)} %get-tuple-element.12), channel_id=1, source_target_pairs={{0,4},{4,0},{1,5},{5,1},{2,6},{6,2},{3,7},{7,3},{8,12},{12,8},{9,1... | collective-permute-start | bytes 3145736 | tf_op jit(solution)/shard_map/ppermute | solution.py:17
  294.9 2.3 copy-start.4
  297.2 3.8 %copy-start.2 = (bf16[16,128,128]{2,1,0:T(8,128)(2,1)S(1)}, bf16[16,128,128]{2,1,0:T(8,128)(2,1)}, u32[]{:S(2)}) copy-start(bf16[16,128,128]{2,1,0:T(8,128)(2,1)} %get-tuple-element.11) | copy-start | bytes 1572868
  301.0 36.5 %copy-start.19 = (f32[16]{0:T(128)S(1)}, f32[16]{0:T(128)}, u32[]{:S(2)}) copy-start(f32[16]{0:T(128)} %get-tuple-element.7) | copy-start | bytes 196
  339.2 1.6 copy-start.1
  340.8 3.3 copy-start.18
  (4 other events, 2.9 us)
Sparse Core Ops, SparseCore 0:
  9.2 29.2 all-gather.10
  40.3 39.4 all-gather.6
  81.7 157.2 all-gather.4
  248.9 26.6 all-gather.8
where the time goes:
time: 353 us; the launch traced here: 352 us
  waiting for transfers between devices  283 us (80%)
  matrix products  27.1 us (8%)
  other arithmetic  14.4 us (4%)
  between operations  13.5 us (4%)
  local copies, waits for them, and re-layouts  8.98 us (3%)
  starting transfers between devices  5.18 us (1%)
    all_gather x1, waiting for transfers between devices, per_device(): lax.all_gather(value_weight, 'dp', axis=0, tiled=True)  156 us
    ppermute x5, waiting for transfers between devices, from_partner(): return lax.ppermute(block, axis, route)  57.7 us
    all_gather x1, waiting for transfers between devices, per_device(): lax.all_gather(lambda_weight, 'dp', axis=0, tiled=True)  39.3 us
    all_gather x1, waiting for transfers between devices, per_device(): lax.all_gather(key_weight, 'dp', axis=0, tiled=True)  28.5 us
    dot_general x4, matrix products, accumulate(): jnp.dot(tokens, piece, preferred_element_type=jnp.float32)  14.8 us
    convert_element_type x3, other arithmetic, per_device(): carried = (carry_decay[:, None, None] * other_state).astype(jnp.bfloat16)  7.3 us
  transfers between devices with their start and end apart: 9, of which 6 were waited for; matrix products, arithmetic and copies ran while one was open for 8% of the time, Pallas kernels for 0%

commit v1 on v0

--- a/solution.py
+++ b/solution.py
@@ -77,6 +77,22 @@
 
 
 def per_device(inputs, query_weight, key_weight, value_weight, lambda_weight, log_decay, norm_gain):
+
+    def serve_strings(packet):
+        n_axis = lax.axis_size("dp")
+        blocks_here = [packet]
+        for m in tuple(range(1, n_axis)):
+            blocks_here.append(
+                lax.ppermute(
+                    blocks_here[m - 1],
+                    axis_name="dp",
+                    perm=[(dev_j, (dev_j - 1) % n_axis) for dev_j in range(n_axis)],
+                )
+            )
+        return jnp.roll(
+            jnp.concatenate(blocks_here, axis=0), lax.axis_index("dp") * packet.shape[0], axis=0
+        )
+
     tokens = inputs[0]
     decays = log_decay[0]
     length = tokens.shape[0]
@@ -85,7 +101,7 @@
         zeros_for(length, (query_weight, key_weight, value_weight, lambda_weight)),
         (
             lax.all_gather(query_weight, "dp", axis=0, tiled=True),
-            lax.all_gather(key_weight, "dp", axis=0, tiled=True),
+            serve_strings(key_weight),
             lax.all_gather(value_weight, "dp", axis=0, tiled=True),
             lax.all_gather(lambda_weight, "dp", axis=0, tiled=True),
         ),

time: 353 us -> 332 us (0.941)
  waiting for transfers between devices: 283 us -> 246 us
  starting transfers between devices: 5.18 us -> 15.8 us
  local copies, waits for them, and re-layouts: 8.98 us -> 14.8 us
    all_gather x1 -> x0, waiting for transfers between devices: 28.5 us -> none  [per_device(): lax.all_gather(key_weight, 'dp', axis=0, tiled=True)]
    all_gather x1, waiting for transfers between devices: 39.3 us -> 13.4 us  [per_device(): lax.all_gather(lambda_weight, 'dp', axis=0, tiled=True)]
    ppermute x0 -> x3, waiting for transfers between devices: none -> 17.9 us  [serve_strings(): lax.ppermute(blocks_here[m - 1], axis_name='dp', perm=[(dev_j, (dev_j - 1...]
    ppermute x0 -> x3, starting transfers between devices: none -> 10.7 us  [serve_strings(): lax.ppermute(blocks_here[m - 1], axis_name='dp', perm=[(dev_j, (dev_j - 1...]
    unnamed x53 -> x62, local copies, waits for them, and re-layouts: 4.71 us -> 9.9 us
  transfers between devices with their start and end apart: 9 -> 11, of which waited for: 6 -> 8; matrix products, arithmetic and copies ran while one was open for 8% -> 11% of each run, Pallas kernels for 0% -> 0%
where the time goes in v1:
time: 332 us
  waiting for transfers between devices  246 us (74%)
  matrix products  27.1 us (8%)
  starting transfers between devices  15.8 us (5%)
  local copies, waits for them, and re-layouts  14.8 us (4%)
  other arithmetic  14.4 us (4%)
  between operations  13.5 us (4%)
    all_gather x1, waiting for transfers between devices, per_device(): lax.all_gather(value_weight, 'dp', axis=0, tiled=True)  156 us
    ppermute x5, waiting for transfers between devices, from_partner(): return lax.ppermute(block, axis, route)  57.8 us
    ppermute x3, waiting for transfers between devices, serve_strings(): lax.ppermute(blocks_here[m - 1], axis_name='dp', perm=[(dev_j, (dev_j - 1...  17.9 us
    dot_general x4, matrix products, accumulate(): jnp.dot(tokens, piece, preferred_element_type=jnp.float32)  14.9 us
    all_gather x1, waiting for transfers between devices, per_device(): lax.all_gather(lambda_weight, 'dp', axis=0, tiled=True)  13.4 us
    ppermute x3, starting transfers between devices, serve_strings(): lax.ppermute(blocks_here[m - 1], axis_name='dp', perm=[(dev_j, (dev_j - 1...  10.7 us
    unnamed x62, local copies, waits for them, and re-layouts  9.9 us
    convert_element_type x3, other arithmetic, per_device(): carried = (carry_decay[:, None, None] * other_state).astype(jnp.bfloat16)  7.29 us
  transfers between devices with their start and end apart: 11, of which 8 were waited for; matrix products, arithmetic and copies ran while one was open for 11% of the time, Pallas kernels for 0%

profile of v1, /device:TPU:0, one launch (start us, length us, event | category | flops | bytes accessed | tf_op | source)
XLA Modules:
  0.0 331.6 jit_solution(5717390410386847655)
XLA Ops:
  8.2 3.9 %collective-permute-start = (bf16[1024,128]{1,0:T(8,128)(2,1)S(1)}, bf16[1024,128]{1,0:T(8,128)(2,1)S(1)}, u32[]{:S(2)}, u32[]{:S(2)}) collective-permute-start(bf16[1024,128]{1,0:T(8,128)(2,1)S(1)} %copy-done.9), channel_id=1, source_target_pairs={{0,24},{8,0},{16,8},{24,16},{1,25},{9,1},{17,9},{25,17},{2,26},{10... | collective-permute-start | bytes 786440 | tf_op jit(solution)/shard_map/ppermute | solution.py:86
  13.4 4.3 %collective-permute-done = bf16[1024,128]{1,0:T(8,128)(2,1)S(1)} collective-permute-done((bf16[1024,128]{1,0:T(8,128)(2,1)S(1)}, bf16[1024,128]{1,0:T(8,128)(2,1)S(1)}, u32[]{:S(2)}, u32[]{:S(2)}) %collective-permute-start) | collective-permute-done | bytes 262176 | tf_op jit(solution)/shard_map/ppermute | solution.py:86
  17.7 3.4 %collective-permute-start.1 = (bf16[1024,128]{1,0:T(8,128)(2,1)S(1)}, bf16[1024,128]{1,0:T(8,128)(2,1)S(1)}, u32[]{:S(2)}, u32[]{:S(2)}) collective-permute-start(bf16[1024,128]{1,0:T(8,128)(2,1)S(1)} %collective-permute-done), channel_id=1, source_target_pairs={{0,24},{8,0},{16,8},{24,16},{1,25},{9,1},{17,9},{25,17},{2,26},{10... | collective-permute-start | bytes 786440 | tf_op jit(solution)/shard_map/ppermute | solution.py:86
  21.4 11.3 %collective-permute-done.1 = bf16[1024,128]{1,0:T(8,128)(2,1)S(1)} collective-permute-done((bf16[1024,128]{1,0:T(8,128)(2,1)S(1)}, bf16[1024,128]{1,0:T(8,128)(2,1)S(1)}, u32[]{:S(2)}, u32[]{:S(2)}) %collective-permute-start.1) | collective-permute-done | bytes 262176 | tf_op jit(solution)/shard_map/ppermute | solution.py:86
  32.7 3.4 %collective-permute-start.2 = (bf16[1024,128]{1,0:T(8,128)(2,1)S(1)}, bf16[1024,128]{1,0:T(8,128)(2,1)S(1)}, u32[]{:S(2)}, u32[]{:S(2)}) collective-permute-start(bf16[1024,128]{1,0:T(8,128)(2,1)S(1)} %collective-permute-done.1), channel_id=1, source_target_pairs={{0,24},{8,0},{16,8},{24,16},{1,25},{9,1},{17,9},{25,17},{2,26},{10... | collective-permute-start | bytes 786440 | tf_op jit(solution)/shard_map/ppermute | solution.py:86
  37.7 2.3 collective-permute-done.2
  43.6 2.1 fusion.21
  45.7 13.4 %all-gather.6.cloned.1.call-done = bf16[4096,320]{0,1:T(8,128)(2,1)} async-done(((bf16[1024,320]{0,1:T(8,128)(2,1)}), bf16[4096,320]{0,1:T(8,128)(2,1)}) %all-gather.6.cloned.1.call-update) | async-done | bytes 2621456 | tf_op jit(solution)/shard_map/all_gather | solution.py:106
  59.0 2.7 compare_select_fusion
  62.6 155.5 %all-gather.4.cloned.1.call-done = bf16[4096,2048]{1,0:T(8,128)(2,1)} async-done(((bf16[1024,2048]{1,0:T(8,128)(2,1)}), bf16[4096,2048]{1,0:T(8,128)(2,1)}) %all-gather.4.cloned.1.call-update) | async-done | bytes 16777232 | tf_op jit(solution)/shard_map/all_gather | solution.py:105
  218.1 8.3 %fusion.15 = bf16[32,16,8,128]{3,2,1,0:T(8,128)(2,1)S(1)} fusion(bf16[4096,2048]{1,0:T(8,128)(2,1)} %all-gather.4.cloned.1.call-done, bf16[1,256,4096]{2,1,0:T(8,128)(2,1)S(1)} %copy-done), kind=kOutput, calls=%fused_computation.22 | convolution fusion | flops 4295491584 | bytes 19922944 | tf_op jit(solution)/shard_map/dot_general | solution.py:69
  226.4 1.0 copy-done.6
  228.5 0.8 convert_add_fusion
  229.3 1.4 collective-permute-done.4
  230.7 3.0 fusion.50
  233.7 1.5 collective-permute-start.5
  237.1 21.9 %collective-permute-done.6 = f32[16]{0:T(128)S(1)} collective-permute-done((f32[16]{0:T(128)S(1)}, f32[16]{0:T(128)S(1)}, u32[]{:S(2)}, u32[]{:S(2)}) %collective-permute-start.6) | collective-permute-done | bytes 96 | tf_op jit(solution)/shard_map/ppermute | solution.py:17
  259.6 1.9 fusion.18
  261.5 0.9 convolution_multiply_fusion
  262.4 2.5 copy.48
  265.0 2.9 multiply_convert_fusion.4
  267.9 2.4 collective-permute-start.7
  270.4 3.4 %fusion.1 = bf16[16,256,256]{2,0,1:T(8,128)(2,1)S(1)} fusion(f32[256,16,9]{2,1,0:T(8,128)S(1)} %copy-done.3, f32[256,256]{1,0:T(8,128)S(1)} %copy-done.10, f32[16,256]{1,0:T(8,128)S(1)} %copy-done.16, f32[16,256]{0,1:T(8,128)S(1)} %copy-done.12, s32[256,256]{1,0:T(8,128)S(1)} %copy-done.11, pred[256,256]{1,0:T(8,128)(4,1)S(1)} %copy-done.17), kind=kOutput, calls=%fused_computation.2 | convolution fusion | flops 119078912 | bytes 2867200 | tf_op jit(solution)/shard_map/lts,thl->hts/dot_general | solution.py:41
  273.8 2.3 fusion.12
  276.1 1.0 copy.42
  277.2 2.8 fusion.52
  280.2 1.8 fusion.53
  282.1 34.6 %collective-permute-done.7 = f32[16,128,128]{2,1,0:T(8,128)} collective-permute-done((f32[16,128,128]{2,1,0:T(8,128)}, f32[16,128,128]{2,1,0:T(8,128)}, u32[]{:S(2)}, u32[]{:S(2)}) %collective-permute-start.7) | collective-permute-done | bytes 1048608 | tf_op jit(solution)/shard_map/ppermute | solution.py:17
  316.6 1.4 multiply_convert_fusion.3
  318.8 1.1 copy-done.1
  319.9 3.3 %multiply_reduce_fusion = (f32[256,16]{0,1:T(8,128)S(1)}, f32[256,16,128]{0,2,1:T(8,128)S(1)}) fusion(f32[256,16]{0,1:T(8,128)S(1)} %copy-done.14, f32[256,16]{0,1:T(8,128)S(1)} %copy-done.13, f32[256,16]{0,1:T(8,128)S(1)} %get-tuple-element.18, f32[16,128,256]{2,1,0:T(8,128)S(1)} %copy-done.1, f32[256,2048]{0,1:S(1)} %fusion.54, f32[256,2048]{0,1} %fusion.53, ...), kind=kLoop, calls=%fused_computation.19 | loop fusion | flops 4190208 | bytes 10551296 | tf_op jit(solution)/shard_map/reduce_sum | solution.py:59
  323.6 1.4 copy.46
  (96 shorter events, 14.3 us)
Async XLA Ops:
  6.5 37.0 %copy-start = (bf16[1,256,4096]{2,1,0:T(8,128)(2,1)S(1)}, bf16[1,256,4096]{2,1,0:T(8,128)(2,1)}, u32[]{:S(2)}) copy-start(bf16[1,256,4096]{2,1,0:T(8,128)(2,1)} %param.7) | copy-start | bytes 6291460
  6.5 52.5 %all-gather.6.cloned.1.call-start = ((), (), s32[]{:S(2)}) async-start(), calls=%async_computation.1 | async-start | bytes 3276800 | tf_op jit(solution)/shard_map/all_gather | solution.py:106
  7.3 4.9 %copy-start.18 = (f32[1,256,16]{1,2,0:T(8,128)S(1)}, f32[1,256,16]{1,2,0:T(8,128)}, u32[]{:S(2)}) copy-start(f32[1,256,16]{1,2,0:T(8,128)} %param.12) | copy-start | bytes 49156
  7.3 210.8 %all-gather.4.cloned.1.call-start = ((), (), s32[]{:S(2)}) async-start(), calls=%async_computation | async-start | bytes 20971520 | tf_op jit(solution)/shard_map/all_gather | solution.py:105
  8.0 251.6 %all-gather.8.cloned.1.call-start = ((), (), s32[]{:S(2)}) async-start(), calls=%async_computation.2 | async-start | bytes 1310720 | tf_op jit(solution)/shard_map/all_gather | solution.py:103
  8.2 9.5 %collective-permute-start = (bf16[1024,128]{1,0:T(8,128)(2,1)S(1)}, bf16[1024,128]{1,0:T(8,128)(2,1)S(1)}, u32[]{:S(2)}, u32[]{:S(2)}) collective-permute-start(bf16[1024,128]{1,0:T(8,128)(2,1)S(1)} %copy-done.9), channel_id=1, source_target_pairs={{0,24},{8,0},{16,8},{24,16},{1,25},{9,1},{17,9},{25,17},{2,26},{10... | collective-permute-start | bytes 786440 | tf_op jit(solution)/shard_map/ppermute | solution.py:86
  17.7 15.0 %collective-permute-start.1 = (bf16[1024,128]{1,0:T(8,128)(2,1)S(1)}, bf16[1024,128]{1,0:T(8,128)(2,1)S(1)}, u32[]{:S(2)}, u32[]{:S(2)}) collective-permute-start(bf16[1024,128]{1,0:T(8,128)(2,1)S(1)} %collective-permute-done), channel_id=1, source_target_pairs={{0,24},{8,0},{16,8},{24,16},{1,25},{9,1},{17,9},{25,17},{2,26},{10... | collective-permute-start | bytes 786440 | tf_op jit(solution)/shard_map/ppermute | solution.py:86
  21.4 215.0 %copy-start.15 = (f32[16,256]{1,0:T(8,128)}, f32[16,256]{1,0:T(8,128)S(1)}, u32[]{:S(2)}) copy-start(f32[16,256]{1,0:T(8,128)S(1)} %get-tuple-element.16) | copy-start | bytes 49156
  32.7 7.3 %collective-permute-start.2 = (bf16[1024,128]{1,0:T(8,128)(2,1)S(1)}, bf16[1024,128]{1,0:T(8,128)(2,1)S(1)}, u32[]{:S(2)}, u32[]{:S(2)}) collective-permute-start(bf16[1024,128]{1,0:T(8,128)(2,1)S(1)} %collective-permute-done.1), channel_id=1, source_target_pairs={{0,24},{8,0},{16,8},{24,16},{1,25},{9,1},{17,9},{25,17},{2,26},{10... | collective-permute-start | bytes 786440 | tf_op jit(solution)/shard_map/ppermute | solution.py:86
  61.8 164.6 %copy-start.5 = (f32[256,16,20]{0,2,1:T(8,128)}, f32[256,16,20]{0,2,1:T(8,128)S(1)}, u32[]{:S(2)}) copy-start(f32[256,16,20]{0,2,1:T(8,128)S(1)} %reshape.113) | copy-start | bytes 983044
  227.8 2.9 copy-start.8
  227.8 2.9 collective-permute-start.3
  227.9 2.7 collective-permute-start.4
  230.7 5.7 %copy-start.21 = (f32[16]{0:T(128)}, f32[16]{0:T(128)S(1)}, u32[]{:S(2)}) copy-start(f32[16]{0:T(128)S(1)} %collective-permute-done.4) | copy-start | bytes 196
  233.7 31.3 %collective-permute-start.5 = (f32[16,128,128]{2,1,0:T(8,128)S(1)}, f32[16,128,128]{2,1,0:T(8,128)}, u32[]{:S(2)}, u32[]{:S(2)}) collective-permute-start(f32[16,128,128]{2,1,0:T(8,128)S(1)} %get-tuple-element.10), channel_id=1, source_target_pairs={{0,2},{2,0},{1,3},{3,1},{4,6},{6,4},{5,7},{7,5},{8,10},{10,8},{9,1... | collective-permute-start | bytes 3145736 | tf_op jit(solution)/shard_map/ppermute | solution.py:17
  235.8 23.8 %copy-start.25 = (f32[16]{0:T(128)}, f32[16]{0:T(128)S(1)}, u32[]{:S(2)}) copy-start(f32[16]{0:T(128)S(1)} %exponential_multiply_fusion) | copy-start | bytes 196
  235.8 23.2 %collective-permute-start.6 = (f32[16]{0:T(128)S(1)}, f32[16]{0:T(128)S(1)}, u32[]{:S(2)}, u32[]{:S(2)}) collective-permute-start(f32[16]{0:T(128)S(1)} %exponential_multiply_fusion), channel_id=1, source_target_pairs={{0,2},{2,0},{1,3},{3,1},{4,6},{6,4},{5,7},{7,5},{8,10},{10,8},{9,1... | collective-permute-start | bytes 200 | tf_op jit(solution)/shard_map/ppermute | solution.py:17
  237.1 25.3 %slice-start = ((f32[256,16,20]{0,2,1:T(8,128)}), f32[256,16,9]{0,2,1:T(8,128)S(1)}, s32[]{:S(2)}) async-start(f32[256,16,20]{0,2,1:T(8,128)} %copy-done.5), calls=%async_computation.3 | async-start | bytes 524288 | tf_op jit(solution)/shard_map/slice | solution.py:41
  262.4 2.6 copy-start.23
  262.4 2.6 copy-start.24
  262.4 2.6 copy-start.26
  265.0 5.4 %copy-start.3 = (f32[256,16,9]{2,1,0:T(8,128)S(1)}, f32[256,16,9]{2,1,0:T(8,128)}, u32[]{:S(2)}) copy-start(f32[256,16,9]{2,1,0:T(8,128)} %copy.48) | copy-start | bytes 442372
  265.0 5.4 %copy-start.10 = (f32[256,256]{1,0:T(8,128)S(1)}, f32[256,256]{1,0:T(8,128)}, u32[]{:S(2)}) copy-start(f32[256,256]{1,0:T(8,128)} %convolution_multiply_fusion) | copy-start | bytes 786436
  265.0 5.4 %copy-start.11 = (s32[256,256]{1,0:T(8,128)S(1)}, s32[256,256]{1,0:T(8,128)}, u32[]{:S(2)}) copy-start(s32[256,256]{1,0:T(8,128)} %convert_add_fusion) | copy-start | bytes 786436
  265.0 5.4 %copy-start.12 = (f32[16,256]{0,1:T(8,128)S(1)}, f32[16,256]{0,1:T(8,128)}, u32[]{:S(2)}) copy-start(f32[16,256]{0,1:T(8,128)} %copy.37) | copy-start | bytes 49156
  265.0 5.4 %copy-start.16 = (f32[16,256]{1,0:T(8,128)S(1)}, f32[16,256]{1,0:T(8,128)}, u32[]{:S(2)}) copy-start(f32[16,256]{1,0:T(8,128)} %copy-done.15) | copy-start | bytes 49156
  265.0 5.4 %copy-start.17 = (pred[256,256]{1,0:T(8,128)(4,1)S(1)}, pred[256,256]{1,0:T(8,128)(4,1)}, u32[]{:S(2)}) copy-start(pred[256,256]{1,0:T(8,128)(4,1)} %iota_compare_fusion.4) | copy-start | bytes 196612
  267.9 5.9 %copy-start.7 = (bf16[32,16,8,128]{3,2,1,0:T(8,128)(2,1)S(1)}, bf16[32,16,8,128]{3,2,1,0:T(8,128)(2,1)}, u32[]{:S(2)}) copy-start(bf16[32,16,8,128]{3,2,1,0:T(8,128)(2,1)} %copy-done.6) | copy-start | bytes 3145732
  267.9 48.7 %collective-permute-start.7 = (f32[16,128,128]{2,1,0:T(8,128)}, f32[16,128,128]{2,1,0:T(8,128)}, u32[]{:S(2)}, u32[]{:S(2)}) collective-permute-start(f32[16,128,128]{2,1,0:T(8,128)} %get-tuple-element.12), channel_id=1, source_target_pairs={{0,4},{4,0},{1,5},{5,1},{2,6},{6,2},{3,7},{7,3},{8,12},{12,8},{9,1... | collective-permute-start | bytes 3145736 | tf_op jit(solution)/shard_map/ppermute | solution.py:17
  276.1 3.8 %copy-start.2 = (bf16[16,128,128]{2,1,0:T(8,128)(2,1)S(1)}, bf16[16,128,128]{2,1,0:T(8,128)(2,1)}, u32[]{:S(2)}) copy-start(bf16[16,128,128]{2,1,0:T(8,128)(2,1)} %get-tuple-element.11) | copy-start | bytes 1572868
  280.0 36.7 %copy-start.20 = (f32[16]{0:T(128)S(1)}, f32[16]{0:T(128)}, u32[]{:S(2)}) copy-start(f32[16]{0:T(128)} %get-tuple-element.7) | copy-start | bytes 196
  319.9 3.3 %copy-start.19 = (f32[2048]{0:T(1024)S(1)}, f32[2048]{0:T(1024)}, u32[]{:S(2)}) copy-start(f32[2048]{0:T(1024)} %param.13) | copy-start | bytes 24580
  (7 other events, 7.9 us)
Sparse Core Ops, SparseCore 0:
  9.2 49.8 all-gather.5
  60.9 157.1 all-gather.3
  228.0 26.6 all-gather.7
